TPU v7x, 32 devices: a whole 2x2x4 slice. The times are simulated.
32 devices in a mesh: row: 8 (over y, x, core), col: 4 (over z).
Axes of the slice: x: 2, y: 2, z: 4, core: 2. Of those that a mesh axis runs over, the one named last changes fastest.
Arguments:
- trial_vectors: bfloat16 [6144, 256], P(('row', 'col')), may hold values from -6 to 6
- h_blocks: bfloat16 [4, 8, 12, 64, 8, 128], P('col', None, None, None, 'row'), may hold values from -0.1875 to 0.1875
- block_col: int32 [4, 8, 12, 8, 2], P('col', 'row'), may hold values from 0 to 2
- block_count: int32 [4, 8, 12, 8], P('col', 'row'), may hold values from 0 to 2, as said below
- center: float32 [1], replicated, may hold values from -0.5 to 0.5
- half_width: float32 [1], replicated, may hold values from 1.5 to 2.5
Outputs:
- filtered: float32 [6144, 256], P(('row', 'col'))
Inputs may be any that keep to these rules, and one draw needn't show every extreme that they name: Only the first block_count slots of a block row and source domain hold blocks. In every column group one row domain has all 2 slots used in every block row for every source domain.
All inputs are finite; a program needn't handle non-finite values.
Results may differ from a plain program's by a relative error of at most 0.019.
Values may be sent and summed in bfloat16 or wider, within the bound.
No kernel may reach another device: no remote copies, remote signals or barrier semaphores. Data moves between devices by JAX's collectives and lax.ppermute only.
A program may use at most 64 MiB of HBM per device.

v0:
```python
import jax
import jax.numpy as jnp
from jax import lax
from jax.sharding import PartitionSpec as P

BLOCK = 64
VECTORS = 256
PER = 2
DEGREE = 6
BLOCK_ROWS = 3


def body(trial_vectors, h_blocks, block_col, block_count, center, half_width):
    arrived = lax.all_to_all(h_blocks, "row", split_axis=1, concat_axis=4, tiled=True)
    row_count = lax.axis_size("row")
    col_count = lax.axis_size("col")
    domain = BLOCK_ROWS * col_count
    filled = (
        lax.broadcasted_iota(jnp.int32, (domain, row_count, PER), 2) < block_count[0, 0][:, :, None]
    )
    shaped = arrived[0, 0].reshape(domain, BLOCK, row_count, PER, BLOCK)
    blocks = jnp.where(filled[:, None, :, :, None], shaped, jnp.zeros((), jnp.bfloat16))
    blocks = blocks.reshape(col_count, BLOCK_ROWS, BLOCK, row_count * PER * BLOCK)
    sources = lax.broadcasted_iota(jnp.int32, (domain, row_count, PER), 1)
    columns = (sources * BLOCK_ROWS + block_col[0, 0]).reshape(
        col_count, BLOCK_ROWS, row_count * PER
    )
    centre_value = center[0]
    half_value = half_width[0]

    def operator(current):
        gathered = lax.all_gather(current, "row", axis=0, tiled=True).reshape(
            row_count * BLOCK_ROWS, BLOCK, VECTORS
        )

        def group_rows(entries):
            group_blocks, group_columns = entries
            picked = gathered[group_columns].reshape(BLOCK_ROWS, row_count * PER * BLOCK, VECTORS)
            return jnp.einsum(
                "rak,rkv->rav", group_blocks, picked, preferred_element_type=jnp.float32
            )

        partial_value = lax.map(group_rows, (blocks, columns)).reshape(domain * BLOCK, VECTORS)
        owned = lax.psum_scatter(
            partial_value.astype(jnp.bfloat16), "col", scatter_dimension=0, tiled=True
        ).astype(jnp.float32)
        return owned

    previous = trial_vectors.astype(jnp.float32)
    current = (operator(trial_vectors) - centre_value * previous) / half_value
    for degree_step in range(DEGREE - 1):
        product = operator(current.astype(jnp.bfloat16))
        following = 2.0 * (product - centre_value * current) / half_value - previous
        previous, current = (current, following)
    return current


def solution(mesh):
    in_specs = (
        P(("row", "col"), None),
        P("col", None, None, None, "row", None),
        P("col", "row", None, None, None),
        P("col", "row", None, None),
        P(),
        P(),
    )
    out_specs = P(("row", "col"), None)
    return jax.shard_map(body, mesh=mesh, in_specs=in_specs, out_specs=out_specs, check_vma=False)
```

profile of v0, /device:TPU:0, one launch (start us, length us, event | category | flops | bytes accessed | tf_op | source)
XLA Modules:
  0.0 303.4 jit_solution(4536157744505953639)
XLA Ops:
  6.5 5.3 %all-to-all-start = ((bf16[1,8,12,64,1,128]{5,3,4,2,0,1:T(8,128)(2,1)}), bf16[1,8,12,64,1,128]{5,3,4,2,0,1:T(8,128)(2,1)S(1)}, u32[]{:S(2)}, u32[]{:S(2)}) async-start(bf16[1,8,12,64,1,128]{5,3,4,2,0,1:T(8,128)(2,1)} %bitcast.176), calls=%async_computation | async-start | bytes 3145728 | tf_op jit(solution)/shard_map/all_to_all | solution.py:14
  12.9 26.2 %all_gather.18 = bf16[1536,256]{1,0:T(8,128)(2,1)} all-gather(bf16[192,256]{1,0:T(8,128)(2,1)S(1)} %copy-done), channel_id=1, replica_groups=mesh['row'=8,'col'=4] {'row'}, dimensions={0}, use_global_device_ids=true | all-gather | bytes 884736 | tf_op jit(solution)/shard_map/all_gather | solution.py:32
  39.1 2.4 copy.27
  41.5 2.5 reshape_squeeze.3
  45.0 11.8 %while.60 = (s32[]{:T(128)}, bf16[4,3,64,256]{3,2,1,0:T(8,128)(2,1)}, bf16[4,3,64,1024]{3,2,1,0:T(8,128)(2,1)S(1)}, s32[4,3,16]{2,0,1:T(4,128)S(1)}, bf16[24,64,256]{2,1,0:T(8,128)(2,1)}, /*index=5*/s32[]{:T(128)}) while((s32[]{:T(128)}, bf16[4,3,64,256]{3,2,1,0:T(8,128)(2,1)}, bf16[4,3,64,1024]{3,2,1,0:T(8,128)(2,1)S(1)}, ...), condition=%wide.region_1.2_spmd, body=%wide.region_0.1_spmd.sunk | while | flops 100664464 | bytes 5314761 | solution.py:43
  45.1 1.8 gather_fusion
  48.0 1.8 gather_fusion
  51.0 1.8 gather_fusion
  53.9 1.8 gather_fusion
  58.1 19.9 %reduce-scatter.7.cloned.1.call-done = bf16[192,256]{1,0:T(8,128)(2,1)} async-done(((bf16[768,256]{1,0:T(8,128)(2,1)}), bf16[192,256]{1,0:T(8,128)(2,1)}) %reduce-scatter.7.cloned.1.call-update) | async-done | bytes 98320 | tf_op jit(solution)/shard_map/reduce_scatter | solution.py:44
  78.9 11.4 %all_gather.19 = bf16[1536,256]{1,0:T(8,128)(2,1)} all-gather(bf16[192,256]{1,0:T(8,128)(2,1)S(1)} %fusion.33), channel_id=1, replica_groups=mesh['row'=8,'col'=4] {'row'}, dimensions={0}, use_global_device_ids=true | all-gather | bytes 884736 | tf_op jit(solution)/shard_map/all_gather | solution.py:32
  91.1 11.8 %while.61 = (s32[]{:T(128)}, bf16[4,3,64,256]{3,2,1,0:T(8,128)(2,1)}, bf16[4,3,64,1024]{3,2,1,0:T(8,128)(2,1)S(1)}, s32[4,3,16]{2,0,1:T(4,128)S(1)}, bf16[24,64,256]{2,1,0:T(8,128)(2,1)}, /*index=5*/s32[]{:T(128)}) while((s32[]{:T(128)}, bf16[4,3,64,256]{3,2,1,0:T(8,128)(2,1)}, bf16[4,3,64,1024]{3,2,1,0:T(8,128)(2,1)S(1)}, ...), condition=%wide.region_4.5_spmd, body=%wide.region_3.4_spmd.sunk | while | flops 100664464 | bytes 5314761 | solution.py:43
  91.2 1.8 gather_fusion.1
  94.1 1.8 gather_fusion.1
  97.1 1.8 gather_fusion.1
  100.0 1.8 gather_fusion.1
  102.9 18.2 %reduce-scatter.9.cloned.1.call-done = bf16[192,256]{1,0:T(8,128)(2,1)} async-done(((bf16[768,256]{1,0:T(8,128)(2,1)}), bf16[192,256]{1,0:T(8,128)(2,1)}) %reduce-scatter.9.cloned.1.call-update) | async-done | bytes 98320 | tf_op jit(solution)/shard_map/reduce_scatter | solution.py:44
  122.1 11.4 %all_gather.20 = bf16[1536,256]{1,0:T(8,128)(2,1)} all-gather(bf16[192,256]{1,0:T(8,128)(2,1)S(1)} %fusion.34), channel_id=1, replica_groups=mesh['row'=8,'col'=4] {'row'}, dimensions={0}, use_global_device_ids=true | all-gather | bytes 884736 | tf_op jit(solution)/shard_map/all_gather | solution.py:32
  134.3 11.8 %while.62 = (s32[]{:T(128)}, bf16[4,3,64,256]{3,2,1,0:T(8,128)(2,1)}, bf16[4,3,64,1024]{3,2,1,0:T(8,128)(2,1)S(1)}, s32[4,3,16]{2,0,1:T(4,128)S(1)}, bf16[24,64,256]{2,1,0:T(8,128)(2,1)}, /*index=5*/s32[]{:T(128)}) while((s32[]{:T(128)}, bf16[4,3,64,256]{3,2,1,0:T(8,128)(2,1)}, bf16[4,3,64,1024]{3,2,1,0:T(8,128)(2,1)S(1)}, ...), condition=%wide.region_7.8_spmd, body=%wide.region_6.7_spmd.sunk | while | flops 100664464 | bytes 5314761 | solution.py:43
  134.4 1.8 gather_fusion.2
  137.4 1.8 gather_fusion.2
  140.3 1.8 gather_fusion.2
  143.2 1.8 gather_fusion.2
  146.1 18.3 %reduce-scatter.11.cloned.1.call-done = bf16[192,256]{1,0:T(8,128)(2,1)} async-done(((bf16[768,256]{1,0:T(8,128)(2,1)}), bf16[192,256]{1,0:T(8,128)(2,1)}) %reduce-scatter.11.cloned.1.call-update) | async-done | bytes 98320 | tf_op jit(solution)/shard_map/reduce_scatter | solution.py:44
  164.4 1.1 fusion.36
  165.4 11.4 %all_gather.21 = bf16[1536,256]{1,0:T(8,128)(2,1)} all-gather(bf16[192,256]{1,0:T(8,128)(2,1)S(1)} %get-tuple-element.325), channel_id=1, replica_groups=mesh['row'=8,'col'=4] {'row'}, dimensions={0}, use_global_device_ids=true | all-gather | bytes 884736 | tf_op jit(solution)/shard_map/all_gather | solution.py:32
  177.6 11.8 %while.63 = (s32[]{:T(128)}, bf16[4,3,64,256]{3,2,1,0:T(8,128)(2,1)}, bf16[4,3,64,1024]{3,2,1,0:T(8,128)(2,1)S(1)}, s32[4,3,16]{2,0,1:T(4,128)S(1)}, bf16[24,64,256]{2,1,0:T(8,128)(2,1)}, /*index=5*/s32[]{:T(128)}) while((s32[]{:T(128)}, bf16[4,3,64,256]{3,2,1,0:T(8,128)(2,1)}, bf16[4,3,64,1024]{3,2,1,0:T(8,128)(2,1)S(1)}, ...), condition=%wide.region_10.11_spmd, body=%wide.region_9.10_spmd.sunk | while | flops 100664464 | bytes 5314761 | solution.py:43
  177.7 1.8 gather_fusion.3
  180.7 1.8 gather_fusion.3
  183.6 1.8 gather_fusion.3
  186.6 1.8 gather_fusion.3
  189.4 18.3 %reduce-scatter.13.cloned.1.call-done = bf16[192,256]{1,0:T(8,128)(2,1)} async-done(((bf16[768,256]{1,0:T(8,128)(2,1)}), bf16[192,256]{1,0:T(8,128)(2,1)}) %reduce-scatter.13.cloned.1.call-update) | async-done | bytes 98320 | tf_op jit(solution)/shard_map/reduce_scatter | solution.py:44
  207.7 1.7 fusion.35
  209.4 11.4 %all_gather.22 = bf16[1536,256]{1,0:T(8,128)(2,1)} all-gather(bf16[192,256]{1,0:T(8,128)(2,1)S(1)} %get-tuple-element.323), channel_id=1, replica_groups=mesh['row'=8,'col'=4] {'row'}, dimensions={0}, use_global_device_ids=true | all-gather | bytes 884736 | tf_op jit(solution)/shard_map/all_gather | solution.py:32
  221.6 11.8 %while.64 = (s32[]{:T(128)}, bf16[4,3,64,256]{3,2,1,0:T(8,128)(2,1)}, bf16[4,3,64,1024]{3,2,1,0:T(8,128)(2,1)S(1)}, s32[4,3,16]{2,0,1:T(4,128)S(1)}, bf16[24,64,256]{2,1,0:T(8,128)(2,1)}, /*index=5*/s32[]{:T(128)}) while((s32[]{:T(128)}, bf16[4,3,64,256]{3,2,1,0:T(8,128)(2,1)}, bf16[4,3,64,1024]{3,2,1,0:T(8,128)(2,1)S(1)}, ...), condition=%wide.region_13.14_spmd, body=%wide.region_12.13_spmd.sunk | while | flops 100664464 | bytes 5314761 | solution.py:43
  221.7 1.8 gather_fusion.4
  224.7 1.8 gather_fusion.4
  227.6 1.8 gather_fusion.4
  230.5 1.8 gather_fusion.4
  233.4 18.3 %reduce-scatter.15.cloned.1.call-done = bf16[192,256]{1,0:T(8,128)(2,1)} async-done(((bf16[768,256]{1,0:T(8,128)(2,1)}), bf16[192,256]{1,0:T(8,128)(2,1)}) %reduce-scatter.15.cloned.1.call-update) | async-done | bytes 98320 | tf_op jit(solution)/shard_map/reduce_scatter | solution.py:44
  252.6 11.4 %all_gather.23 = bf16[1536,256]{1,0:T(8,128)(2,1)} all-gather(bf16[192,256]{1,0:T(8,128)(2,1)S(1)} %fusion.32), channel_id=1, replica_groups=mesh['row'=8,'col'=4] {'row'}, dimensions={0}, use_global_device_ids=true | all-gather | bytes 884736 | tf_op jit(solution)/shard_map/all_gather | solution.py:32
  264.8 11.8 %while.65 = (s32[]{:T(128)}, bf16[4,3,64,256]{3,2,1,0:T(8,128)(2,1)}, bf16[4,3,64,1024]{3,2,1,0:T(8,128)(2,1)S(1)}, s32[4,3,16]{2,0,1:T(4,128)S(1)}, bf16[24,64,256]{2,1,0:T(8,128)(2,1)}, /*index=5*/s32[]{:T(128)}) while((s32[]{:T(128)}, bf16[4,3,64,256]{3,2,1,0:T(8,128)(2,1)}, bf16[4,3,64,1024]{3,2,1,0:T(8,128)(2,1)S(1)}, ...), condition=%wide.region_16.17_spmd, body=%wide.region_15.16_spmd.sunk | while | flops 100664464 | bytes 5314761 | solution.py:43
  264.9 1.8 gather_fusion.5
  267.9 1.8 gather_fusion.5
  270.8 1.8 gather_fusion.5
  273.7 1.8 gather_fusion.5
  276.6 18.3 %reduce-scatter.17.cloned.1.call-done = bf16[192,256]{1,0:T(8,128)(2,1)} async-done(((bf16[768,256]{1,0:T(8,128)(2,1)}), bf16[192,256]{1,0:T(8,128)(2,1)}) %reduce-scatter.17.cloned.1.call-update) | async-done | bytes 98320 | tf_op jit(solution)/shard_map/reduce_scatter | solution.py:44
  294.9 1.7 divide_subtract_fusion
  (139 shorter events, 36.1 us)
Async XLA Ops:
  6.5 5.4 %copy-start.4 = (s32[1,1,12,8]{2,3,1,0:T(8,128)S(1)}, s32[1,1,12,8]{2,3,1,0:T(8,128)}, u32[]{:S(2)}) copy-start(s32[1,1,12,8]{2,3,1,0:T(8,128)} %param.21) | copy-start | bytes 1156
  6.5 5.9 %copy-start.3 = (s32[1,1,12,8,2]{2,4,3,1,0:T(2,128)S(1)}, s32[1,1,12,8,2]{2,4,3,1,0:T(2,128)}, u32[]{:S(2)}) copy-start(s32[1,1,12,8,2]{2,4,3,1,0:T(2,128)} %param.20) | copy-start | bytes 2308
  6.5 6.3 %copy-start = (bf16[192,256]{1,0:T(8,128)(2,1)S(1)}, bf16[192,256]{1,0:T(8,128)(2,1)}, u32[]{:S(2)}) copy-start(bf16[192,256]{1,0:T(8,128)(2,1)} %param.18) | copy-start | bytes 294916
  6.5 32.6 %all-to-all-start = ((bf16[1,8,12,64,1,128]{5,3,4,2,0,1:T(8,128)(2,1)}), bf16[1,8,12,64,1,128]{5,3,4,2,0,1:T(8,128)(2,1)S(1)}, u32[]{:S(2)}, u32[]{:S(2)}) async-start(bf16[1,8,12,64,1,128]{5,3,4,2,0,1:T(8,128)(2,1)} %bitcast.176), calls=%async_computation | async-start | bytes 3145728 | tf_op jit(solution)/shard_map/all_to_all | solution.py:14
  11.9 66.1 %reduce-scatter.7.cloned.1.call-start = ((), (), s32[]{:S(2)}) async-start(), calls=%async_computation.7 | async-start | bytes 491520 | tf_op jit(solution)/shard_map/reduce_scatter | solution.py:44
  56.8 64.4 %reduce-scatter.9.cloned.1.call-start = ((), (), s32[]{:S(2)}) async-start(), calls=%async_computation.8 | async-start | bytes 491520 | tf_op jit(solution)/shard_map/reduce_scatter | solution.py:44
  91.1 30.1 %copy-start.2 = (bf16[192,256]{1,0:T(8,128)(2,1)S(1)}, bf16[192,256]{1,0:T(8,128)(2,1)}, u32[]{:S(2)}) copy-start(bf16[192,256]{1,0:T(8,128)(2,1)} %reduce-scatter.7.cloned.1.call-done) | copy-start | bytes 294916
  102.9 61.5 %reduce-scatter.11.cloned.1.call-start = ((), (), s32[]{:S(2)}) async-start(), calls=%async_computation.9 | async-start | bytes 491520 | tf_op jit(solution)/shard_map/reduce_scatter | solution.py:44
  146.1 61.6 %reduce-scatter.13.cloned.1.call-start = ((), (), s32[]{:S(2)}) async-start(), calls=%async_computation.10 | async-start | bytes 491520 | tf_op jit(solution)/shard_map/reduce_scatter | solution.py:44
  189.4 62.3 %reduce-scatter.15.cloned.1.call-start = ((), (), s32[]{:S(2)}) async-start(), calls=%async_computation.11 | async-start | bytes 491520 | tf_op jit(solution)/shard_map/reduce_scatter | solution.py:44
  221.6 30.1 %copy-start.1 = (f32[192,256]{1,0:T(8,128)S(1)}, f32[192,256]{1,0:T(8,128)}, u32[]{:S(2)}) copy-start(f32[192,256]{1,0:T(8,128)} %get-tuple-element.324) | copy-start | bytes 589828
  233.4 61.5 %reduce-scatter.17.cloned.1.call-start = ((), (), s32[]{:S(2)}) async-start(), calls=%async_computation.12 | async-start | bytes 491520 | tf_op jit(solution)/shard_map/reduce_scatter | solution.py:44
Sparse Core Ops, SparseCore 0:
  56.9 21.0 reduce-scatter.6
  103.0 18.1 reduce-scatter.8
  146.2 18.1 reduce-scatter.10
  189.5 18.1 reduce-scatter.12
  233.5 18.1 reduce-scatter.14
  276.7 18.1 reduce-scatter.16
where the time goes:
time: 305 us; the launch traced here: 303 us
  waiting for transfers between devices  111 us (36%)
  blocking collectives  83.1 us (27%)
  local copies, waits for them, and re-layouts  55.5 us (18%)
  matrix products  24.4 us (8%)
  between operations  14.9 us (5%)
  other arithmetic  8.43 us (3%)
  starting transfers between devices  5.57 us (2%)
    reduce_scatter x6, waiting for transfers between devices, operator(): lax.psum_scatter(partial_value.astype(jnp.bfloat16), 'col', scatter_dimen...  111 us
    all_gather x6, blocking collectives, operator(): lax.all_gather(current, 'row', axis=0, tiled=True)  83.1 us
    gather x24, local copies, waits for them, and re-layouts, group_rows(): gathered[group_columns]  43 us
    dot_general x24, matrix products, group_rows(): jnp.einsum('rak,rkv->rav', group_blocks, picked, preferred_element_type=j...  24.4 us
  transfers between devices with their start and end apart: 7, of which 6 were waited for; matrix products, arithmetic and copies ran while one was open for 0% of the time, Pallas kernels for 0%

commit v1 on v0

--- a/solution.py
+++ b/solution.py
@@ -8,6 +8,30 @@
 PER = 2
 DEGREE = 6
 BLOCK_ROWS = 3
+
+
+def match_loads_now(d_out, vals):
+    far_arr = lax.axis_size("row")
+    f_next = lax.axis_index("row")
+    front, back, odd = (far_arr, f_next, vals.shape[d_out])
+    nodes = [dev * front if h == d_out else dev for h, dev in enumerate(vals.shape)]
+    w1 = lax.dynamic_update_slice_in_dim(jnp.zeros(nodes, vals.dtype), vals, back * odd, axis=d_out)
+    m_next = part_next = vals
+    for m in range(1, front // 2 + 1):
+        m_next = lax.ppermute(
+            m_next, axis_name="row", perm=list(map(lambda h: (h, (h + 1) % front), range(front)))
+        )
+        w1 = lax.dynamic_update_slice_in_dim(w1, m_next, (back - m) % front * odd, axis=d_out)
+        if 2 * m < front:
+            part_next = lax.ppermute(
+                part_next,
+                axis_name="row",
+                perm=list(map(lambda h: (h, (h - 1) % front), range(front))),
+            )
+            w1 = lax.dynamic_update_slice_in_dim(
+                w1, part_next, (back + m) % front * odd, axis=d_out
+            )
+    return w1
 
 
 def body(trial_vectors, h_blocks, block_col, block_count, center, half_width):
@@ -29,9 +53,7 @@
     half_value = half_width[0]
 
     def operator(current):
-        gathered = lax.all_gather(current, "row", axis=0, tiled=True).reshape(
-            row_count * BLOCK_ROWS, BLOCK, VECTORS
-        )
+        gathered = match_loads_now(0, current).reshape(row_count * BLOCK_ROWS, BLOCK, VECTORS)
 
         def group_rows(entries):
             group_blocks, group_columns = entries

time: 305 us -> 371 us (1.22)
  blocking collectives: 83.1 us -> 0 us
  waiting for transfers between devices: 111 us -> 183 us
  starting transfers between devices: 5.57 us -> 53.1 us
  local copies, waits for them, and re-layouts: 55.5 us -> 83.7 us
    all_gather x6 -> x0, blocking collectives: 83.1 us -> none  [operator(): lax.all_gather(current, 'row', axis=0, tiled=True)]
    ppermute x0 -> x42, waiting for transfers between devices: none -> 66.3 us  [the longest x24 62.2 us: match_loads_now(): lax.ppermute(m_next, axis_name='row', perm=list(map(lambda h: (h, (h + 1)...]
    ppermute x0 -> x42, starting transfers between devices: none -> 49.1 us  [the longest x18 48.2 us: match_loads_now(): lax.ppermute(part_next, axis_name='row', perm=list(map(lambda h: (h, (h -...]
    dynamic_update_slice x0 -> x43, local copies, waits for them, and re-layouts: none -> 23.1 us  [the longest x24 12.8 us: match_loads_now(): lax.dynamic_update_slice_in_dim(w1, m_next, (back - m) % front * odd, axi...]
    dynamic_update_slice x0 -> x5, other arithmetic: none -> 7.53 us  [match_loads_now(): lax.dynamic_update_slice_in_dim(jnp.zeros(nodes, vals.dtype), vals, back...]
    convert_element_type x5 -> x0, other arithmetic: 5.64 us -> none  [body(): product = operator(current.astype(jnp.bfloat16))]
    reduce_scatter x6, waiting for transfers between devices: 111 us -> 116 us  [operator(): lax.psum_scatter(partial_value.astype(jnp.bfloat16), 'col', scatter_dimen...]
    another operation x6 -> x12, local copies, waits for them, and re-layouts: 4.67 us -> 9.56 us
  transfers between devices with their start and end apart: 7 -> 49, of which waited for: 6 -> 38; matrix products, arithmetic and copies ran while one was open for 0% -> 6% of each run, Pallas kernels for 0% -> 0%
where the time goes in v1:
time: 371 us; the launch traced here: 370 us
  waiting for transfers between devices  183 us (49%)
  local copies, waits for them, and re-layouts  83.7 us (23%)
  starting transfers between devices  53.1 us (14%)
  matrix products  24.5 us (7%)
  between operations  15.1 us (4%)
  other arithmetic  10.3 us (3%)
    reduce_scatter x6, waiting for transfers between devices, operator(): lax.psum_scatter(partial_value.astype(jnp.bfloat16), 'col', scatter_dimen...  116 us
    ppermute x24, waiting for transfers between devices, match_loads_now(): lax.ppermute(m_next, axis_name='row', perm=list(map(lambda h: (h, (h + 1)...  62.2 us
    ppermute x18, starting transfers between devices, match_loads_now(): lax.ppermute(part_next, axis_name='row', perm=list(map(lambda h: (h, (h -...  48.2 us
    gather x24, local copies, waits for them, and re-layouts, group_rows(): gathered[group_columns]  43 us
    dot_general x24, matrix products, group_rows(): jnp.einsum('rak,rkv->rav', group_blocks, picked, preferred_element_type=j...  24.5 us
    dynamic_update_slice x24, local copies, waits for them, and re-layouts, match_loads_now(): lax.dynamic_update_slice_in_dim(w1, m_next, (back - m) % front * odd, axi...  12.8 us
    dynamic_update_slice x18, local copies, waits for them, and re-layouts, match_loads_now(): lax.dynamic_update_slice_in_dim(w1, part_next, (back + m) % front * odd,...  9.65 us
    another operation x12, local copies, waits for them, and re-layouts  9.56 us
  transfers between devices with their start and end apart: 49, of which 38 were waited for; matrix products, arithmetic and copies ran while one was open for 6% of the time, Pallas kernels for 0%

profile of v1, /device:TPU:0, one launch (start us, length us, event | category | flops | bytes accessed | tf_op | source)
XLA Modules:
  0.0 369.5 jit_solution(1182048212100793228)
XLA Ops:
  7.0 2.9 collective-permute-start.1
  9.9 3.7 %all-to-all-start = ((bf16[1,8,12,64,1,128]{5,3,4,2,0,1:T(8,128)(2,1)}), bf16[1,8,12,64,1,128]{5,3,4,2,0,1:T(8,128)(2,1)S(1)}, u32[]{:S(2)}, u32[]{:S(2)}) async-start(bf16[1,8,12,64,1,128]{5,3,4,2,0,1:T(8,128)(2,1)} %bitcast.171), calls=%async_computation | async-start | bytes 3145728 | tf_op jit(solution)/shard_map/all_to_all | solution.py:38
  16.6 2.3 collective-permute-start.3
  20.3 15.9 %collective-permute-done.2 = bf16[192,256]{1,0:T(8,128)(2,1)S(1)} collective-permute-done((bf16[192,256]{1,0:T(8,128)(2,1)S(1)}, bf16[192,256]{1,0:T(8,128)(2,1)S(1)}, u32[]{:S(2)}, u32[]{:S(2)}) %collective-permute-start.2) | collective-permute-done | bytes 98336 | tf_op jit(solution)/shard_map/ppermute | solution.py:21
  36.2 2.6 collective-permute-start.5
  40.1 1.9 collective-permute-done.4
  43.3 3.7 collective-permute-done.6
  47.6 2.4 copy.27
  50.0 2.5 reshape_squeeze.3
  53.5 11.8 %while.60 = (s32[]{:T(128)}, bf16[4,3,64,256]{3,2,1,0:T(8,128)(2,1)}, bf16[4,3,64,1024]{3,2,1,0:T(8,128)(2,1)S(1)}, s32[4,3,16]{2,0,1:T(4,128)S(1)}, bf16[24,64,256]{2,1,0:T(8,128)(2,1)}, /*index=5*/s32[]{:T(128)}) while((s32[]{:T(128)}, bf16[4,3,64,256]{3,2,1,0:T(8,128)(2,1)}, bf16[4,3,64,1024]{3,2,1,0:T(8,128)(2,1)S(1)}, ...), condition=%wide.region_1.2_spmd, body=%wide.region_0.1_spmd.sunk | while | flops 100664464 | bytes 5314761 | solution.py:65
  66.6 19.8 %reduce-scatter.7.cloned.1.call-done = bf16[192,256]{1,0:T(8,128)(2,1)} async-done(((bf16[768,256]{1,0:T(8,128)(2,1)}), bf16[192,256]{1,0:T(8,128)(2,1)}) %reduce-scatter.7.cloned.1.call-update) | async-done | bytes 98320 | tf_op jit(solution)/shard_map/reduce_scatter | solution.py:66
  88.9 2.6 collective-permute-start.8
  91.6 2.3 collective-permute-done.7
  94.5 2.6 collective-permute-start.10
  99.6 2.8 collective-permute-start.12
  106.1 2.8 collective-permute-done.13
  110.3 11.8 %while.61 = (s32[]{:T(128)}, bf16[4,3,64,256]{3,2,1,0:T(8,128)(2,1)}, bf16[4,3,64,1024]{3,2,1,0:T(8,128)(2,1)S(1)}, s32[4,3,16]{2,0,1:T(4,128)S(1)}, bf16[24,64,256]{2,1,0:T(8,128)(2,1)}, /*index=5*/s32[]{:T(128)}) while((s32[]{:T(128)}, bf16[4,3,64,256]{3,2,1,0:T(8,128)(2,1)}, bf16[4,3,64,1024]{3,2,1,0:T(8,128)(2,1)S(1)}, ...), condition=%wide.region_4.5_spmd, body=%wide.region_3.4_spmd.sunk | while | flops 100664464 | bytes 5314761 | solution.py:65
  122.2 19.5 %reduce-scatter.9.cloned.1.call-done = bf16[192,256]{1,0:T(8,128)(2,1)} async-done(((bf16[768,256]{1,0:T(8,128)(2,1)}), bf16[192,256]{1,0:T(8,128)(2,1)}) %reduce-scatter.9.cloned.1.call-update) | async-done | bytes 98320 | tf_op jit(solution)/shard_map/reduce_scatter | solution.py:66
  144.2 2.6 collective-permute-start.15
  146.9 2.3 collective-permute-done.14
  149.8 2.6 collective-permute-start.17
  154.9 2.8 collective-permute-start.19
  161.4 2.8 collective-permute-done.20
  165.6 11.8 %while.62 = (s32[]{:T(128)}, bf16[4,3,64,256]{3,2,1,0:T(8,128)(2,1)}, bf16[4,3,64,1024]{3,2,1,0:T(8,128)(2,1)S(1)}, s32[4,3,16]{2,0,1:T(4,128)S(1)}, bf16[24,64,256]{2,1,0:T(8,128)(2,1)}, /*index=5*/s32[]{:T(128)}) while((s32[]{:T(128)}, bf16[4,3,64,256]{3,2,1,0:T(8,128)(2,1)}, bf16[4,3,64,1024]{3,2,1,0:T(8,128)(2,1)S(1)}, ...), condition=%wide.region_7.8_spmd, body=%wide.region_6.7_spmd.sunk | while | flops 100664464 | bytes 5314761 | solution.py:65
  177.4 19.6 %reduce-scatter.11.cloned.1.call-done = bf16[192,256]{1,0:T(8,128)(2,1)} async-done(((bf16[768,256]{1,0:T(8,128)(2,1)}), bf16[192,256]{1,0:T(8,128)(2,1)}) %reduce-scatter.11.cloned.1.call-update) | async-done | bytes 98320 | tf_op jit(solution)/shard_map/reduce_scatter | solution.py:66
  199.7 2.6 collective-permute-start.22
  202.3 2.3 collective-permute-done.21
  205.2 2.6 collective-permute-start.24
  210.4 2.8 collective-permute-start.26
  216.8 2.8 collective-permute-done.27
  221.1 11.8 %while.63 = (s32[]{:T(128)}, bf16[4,3,64,256]{3,2,1,0:T(8,128)(2,1)}, bf16[4,3,64,1024]{3,2,1,0:T(8,128)(2,1)S(1)}, s32[4,3,16]{2,0,1:T(4,128)S(1)}, bf16[24,64,256]{2,1,0:T(8,128)(2,1)}, /*index=5*/s32[]{:T(128)}) while((s32[]{:T(128)}, bf16[4,3,64,256]{3,2,1,0:T(8,128)(2,1)}, bf16[4,3,64,1024]{3,2,1,0:T(8,128)(2,1)S(1)}, ...), condition=%wide.region_10.11_spmd, body=%wide.region_9.10_spmd.sunk | while | flops 100664464 | bytes 5314761 | solution.py:65
  232.9 19.5 %reduce-scatter.13.cloned.1.call-done = bf16[192,256]{1,0:T(8,128)(2,1)} async-done(((bf16[768,256]{1,0:T(8,128)(2,1)}), bf16[192,256]{1,0:T(8,128)(2,1)}) %reduce-scatter.13.cloned.1.call-update) | async-done | bytes 98320 | tf_op jit(solution)/shard_map/reduce_scatter | solution.py:66
  255.1 2.6 collective-permute-start.29
  257.7 2.3 collective-permute-done.28
  260.7 2.6 collective-permute-start.31
  265.8 2.8 collective-permute-start.33
  272.2 2.8 collective-permute-done.34
  276.5 11.8 %while.64 = (s32[]{:T(128)}, bf16[4,3,64,256]{3,2,1,0:T(8,128)(2,1)}, bf16[4,3,64,1024]{3,2,1,0:T(8,128)(2,1)S(1)}, s32[4,3,16]{2,0,1:T(4,128)S(1)}, bf16[24,64,256]{2,1,0:T(8,128)(2,1)}, /*index=5*/s32[]{:T(128)}) while((s32[]{:T(128)}, bf16[4,3,64,256]{3,2,1,0:T(8,128)(2,1)}, bf16[4,3,64,1024]{3,2,1,0:T(8,128)(2,1)S(1)}, ...), condition=%wide.region_13.14_spmd, body=%wide.region_12.13_spmd.sunk | while | flops 100664464 | bytes 5314761 | solution.py:65
  288.3 19.6 %reduce-scatter.15.cloned.1.call-done = bf16[192,256]{1,0:T(8,128)(2,1)} async-done(((bf16[768,256]{1,0:T(8,128)(2,1)}), bf16[192,256]{1,0:T(8,128)(2,1)}) %reduce-scatter.15.cloned.1.call-update) | async-done | bytes 98320 | tf_op jit(solution)/shard_map/reduce_scatter | solution.py:66
  309.0 2.6 collective-permute-start.36
  311.6 2.3 collective-permute-done.35
  313.9 2.7 collective-permute-start.38
  316.6 2.5 collective-permute-done.37
  319.1 2.7 collective-permute-start.40
  321.9 3.1 collective-permute-done.39
  325.0 4.8 %collective-permute-done.41 = bf16[192,256]{1,0:T(8,128)(2,1)S(1)} collective-permute-done((bf16[192,256]{1,0:T(8,128)(2,1)S(1)}, bf16[192,256]{1,0:T(8,128)(2,1)S(1)}, u32[]{:S(2)}, u32[]{:S(2)}) %collective-permute-start.41) | collective-permute-done | bytes 98336 | tf_op jit(solution)/shard_map/ppermute | solution.py:21
  330.9 11.8 %while.65 = (s32[]{:T(128)}, bf16[4,3,64,256]{3,2,1,0:T(8,128)(2,1)}, bf16[4,3,64,1024]{3,2,1,0:T(8,128)(2,1)S(1)}, s32[4,3,16]{2,0,1:T(4,128)S(1)}, bf16[24,64,256]{2,1,0:T(8,128)(2,1)}, /*index=5*/s32[]{:T(128)}) while((s32[]{:T(128)}, bf16[4,3,64,256]{3,2,1,0:T(8,128)(2,1)}, bf16[4,3,64,1024]{3,2,1,0:T(8,128)(2,1)S(1)}, ...), condition=%wide.region_16.17_spmd, body=%wide.region_15.16_spmd.sunk | while | flops 100664464 | bytes 5314761 | solution.py:65
  342.7 18.3 %reduce-scatter.17.cloned.1.call-done = bf16[192,256]{1,0:T(8,128)(2,1)} async-done(((bf16[768,256]{1,0:T(8,128)(2,1)}), bf16[192,256]{1,0:T(8,128)(2,1)}) %reduce-scatter.17.cloned.1.call-update) | async-done | bytes 98320 | tf_op jit(solution)/shard_map/reduce_scatter | solution.py:66
  (268 shorter events, 126.4 us)
Async XLA Ops:
  6.5 9.8 %collective-permute-start = (bf16[192,256]{1,0:T(8,128)(2,1)}, bf16[192,256]{1,0:T(8,128)(2,1)S(1)}, u32[]{:S(2)}, u32[]{:S(2)}) collective-permute-start(bf16[192,256]{1,0:T(8,128)(2,1)} %param.18), channel_id=1, source_target_pairs={{0,4},{4,8},{8,12},{12,16},{16,20},{20,24},{24,28},{28,0},{1,5},{5... | collective-permute-start | bytes 294920 | tf_op jit(solution)/shard_map/ppermute | solution.py:21
  7.0 9.6 %collective-permute-start.1 = (bf16[192,256]{1,0:T(8,128)(2,1)}, bf16[192,256]{1,0:T(8,128)(2,1)S(1)}, u32[]{:S(2)}, u32[]{:S(2)}) collective-permute-start(bf16[192,256]{1,0:T(8,128)(2,1)} %param.18), channel_id=1, source_target_pairs={{0,28},{4,0},{8,4},{12,8},{16,12},{20,16},{24,20},{28,24},{1,29},{... | collective-permute-start | bytes 294920 | tf_op jit(solution)/shard_map/ppermute | solution.py:26
  9.9 37.7 %all-to-all-start = ((bf16[1,8,12,64,1,128]{5,3,4,2,0,1:T(8,128)(2,1)}), bf16[1,8,12,64,1,128]{5,3,4,2,0,1:T(8,128)(2,1)S(1)}, u32[]{:S(2)}, u32[]{:S(2)}) async-start(bf16[1,8,12,64,1,128]{5,3,4,2,0,1:T(8,128)(2,1)} %bitcast.171), calls=%async_computation | async-start | bytes 3145728 | tf_op jit(solution)/shard_map/all_to_all | solution.py:38
  13.6 72.8 %reduce-scatter.7.cloned.1.call-start = ((), (), s32[]{:S(2)}) async-start(), calls=%async_computation.7 | async-start | bytes 491520 | tf_op jit(solution)/shard_map/reduce_scatter | solution.py:66
  16.3 19.8 %collective-permute-start.2 = (bf16[192,256]{1,0:T(8,128)(2,1)S(1)}, bf16[192,256]{1,0:T(8,128)(2,1)S(1)}, u32[]{:S(2)}, u32[]{:S(2)}) collective-permute-start(bf16[192,256]{1,0:T(8,128)(2,1)S(1)} %collective-permute-done), channel_id=1, source_target_pairs={{0,4},{4,8},{8,12},{12,16},{16,20},{20,24},{24,28},{28,0},{1,5},{5... | collective-permute-start | bytes 294920 | tf_op jit(solution)/shard_map/ppermute | solution.py:21
  16.6 19.5 %collective-permute-start.3 = (bf16[192,256]{1,0:T(8,128)(2,1)S(1)}, bf16[192,256]{1,0:T(8,128)(2,1)S(1)}, u32[]{:S(2)}, u32[]{:S(2)}) collective-permute-start(bf16[192,256]{1,0:T(8,128)(2,1)S(1)} %collective-permute-done.1), channel_id=1, source_target_pairs={{0,28},{4,0},{8,4},{12,8},{16,12},{20,16},{24,20},{28,24},{1,29},{... | collective-permute-start | bytes 294920 | tf_op jit(solution)/shard_map/ppermute | solution.py:26
  36.1 5.8 %collective-permute-start.4 = (bf16[192,256]{1,0:T(8,128)(2,1)S(1)}, bf16[192,256]{1,0:T(8,128)(2,1)S(1)}, u32[]{:S(2)}, u32[]{:S(2)}) collective-permute-start(bf16[192,256]{1,0:T(8,128)(2,1)S(1)} %collective-permute-done.2), channel_id=1, source_target_pairs={{0,4},{4,8},{8,12},{12,16},{16,20},{20,24},{24,28},{28,0},{1,5},{5... | collective-permute-start | bytes 294920 | tf_op jit(solution)/shard_map/ppermute | solution.py:21
  36.2 6.5 %collective-permute-start.5 = (bf16[192,256]{1,0:T(8,128)(2,1)S(1)}, bf16[192,256]{1,0:T(8,128)(2,1)S(1)}, u32[]{:S(2)}, u32[]{:S(2)}) collective-permute-start(bf16[192,256]{1,0:T(8,128)(2,1)S(1)} %collective-permute-done.3), channel_id=1, source_target_pairs={{0,28},{4,0},{8,4},{12,8},{16,12},{20,16},{24,20},{28,24},{1,29},{... | collective-permute-start | bytes 294920 | tf_op jit(solution)/shard_map/ppermute | solution.py:26
  42.0 4.9 %collective-permute-start.6 = (bf16[192,256]{1,0:T(8,128)(2,1)S(1)}, bf16[192,256]{1,0:T(8,128)(2,1)S(1)}, u32[]{:S(2)}, u32[]{:S(2)}) collective-permute-start(bf16[192,256]{1,0:T(8,128)(2,1)S(1)} %collective-permute-done.4), channel_id=1, source_target_pairs={{0,4},{4,8},{8,12},{12,16},{16,20},{20,24},{24,28},{28,0},{1,5},{5... | collective-permute-start | bytes 294920 | tf_op jit(solution)/shard_map/ppermute | solution.py:21
  65.3 76.4 %reduce-scatter.9.cloned.1.call-start = ((), (), s32[]{:S(2)}) async-start(), calls=%async_computation.8 | async-start | bytes 491520 | tf_op jit(solution)/shard_map/reduce_scatter | solution.py:66
  88.9 4.9 %collective-permute-start.7 = (bf16[192,256]{1,0:T(8,128)(2,1)S(1)}, bf16[192,256]{1,0:T(8,128)(2,1)S(1)}, u32[]{:S(2)}, u32[]{:S(2)}) collective-permute-start(bf16[192,256]{1,0:T(8,128)(2,1)S(1)} %get-tuple-element.334), channel_id=1, source_target_pairs={{0,4},{4,8},{8,12},{12,16},{16,20},{20,24},{24,28},{28,0},{1,5},{5... | collective-permute-start | bytes 294920 | tf_op jit(solution)/shard_map/ppermute | solution.py:21
  88.9 5.6 %collective-permute-start.8 = (bf16[192,256]{1,0:T(8,128)(2,1)S(1)}, bf16[192,256]{1,0:T(8,128)(2,1)S(1)}, u32[]{:S(2)}, u32[]{:S(2)}) collective-permute-start(bf16[192,256]{1,0:T(8,128)(2,1)S(1)} %get-tuple-element.334), channel_id=1, source_target_pairs={{0,28},{4,0},{8,4},{12,8},{16,12},{20,16},{24,20},{28,24},{1,29},{... | collective-permute-start | bytes 294920 | tf_op jit(solution)/shard_map/ppermute | solution.py:26
  93.9 4.9 %collective-permute-start.9 = (bf16[192,256]{1,0:T(8,128)(2,1)S(1)}, bf16[192,256]{1,0:T(8,128)(2,1)S(1)}, u32[]{:S(2)}, u32[]{:S(2)}) collective-permute-start(bf16[192,256]{1,0:T(8,128)(2,1)S(1)} %collective-permute-done.7), channel_id=1, source_target_pairs={{0,4},{4,8},{8,12},{12,16},{16,20},{20,24},{24,28},{28,0},{1,5},{5... | collective-permute-start | bytes 294920 | tf_op jit(solution)/shard_map/ppermute | solution.py:21
  94.5 5.1 %collective-permute-start.10 = (bf16[192,256]{1,0:T(8,128)(2,1)S(1)}, bf16[192,256]{1,0:T(8,128)(2,1)S(1)}, u32[]{:S(2)}, u32[]{:S(2)}) collective-permute-start(bf16[192,256]{1,0:T(8,128)(2,1)S(1)} %collective-permute-done.8), channel_id=1, source_target_pairs={{0,28},{4,0},{8,4},{12,8},{16,12},{20,16},{24,20},{28,24},{1,29},{... | collective-permute-start | bytes 294920 | tf_op jit(solution)/shard_map/ppermute | solution.py:26
  98.8 5.1 %collective-permute-start.11 = (bf16[192,256]{1,0:T(8,128)(2,1)S(1)}, bf16[192,256]{1,0:T(8,128)(2,1)S(1)}, u32[]{:S(2)}, u32[]{:S(2)}) collective-permute-start(bf16[192,256]{1,0:T(8,128)(2,1)S(1)} %collective-permute-done.9), channel_id=1, source_target_pairs={{0,4},{4,8},{8,12},{12,16},{16,20},{20,24},{24,28},{28,0},{1,5},{5... | collective-permute-start | bytes 294920 | tf_op jit(solution)/shard_map/ppermute | solution.py:21
  99.6 5.9 %collective-permute-start.12 = (bf16[192,256]{1,0:T(8,128)(2,1)S(1)}, bf16[192,256]{1,0:T(8,128)(2,1)S(1)}, u32[]{:S(2)}, u32[]{:S(2)}) collective-permute-start(bf16[192,256]{1,0:T(8,128)(2,1)S(1)} %collective-permute-done.10), channel_id=1, source_target_pairs={{0,28},{4,0},{8,4},{12,8},{16,12},{20,16},{24,20},{28,24},{1,29},{... | collective-permute-start | bytes 294920 | tf_op jit(solution)/shard_map/ppermute | solution.py:26
  104.0 4.9 %collective-permute-start.13 = (bf16[192,256]{1,0:T(8,128)(2,1)S(1)}, bf16[192,256]{1,0:T(8,128)(2,1)S(1)}, u32[]{:S(2)}, u32[]{:S(2)}) collective-permute-start(bf16[192,256]{1,0:T(8,128)(2,1)S(1)} %collective-permute-done.11), channel_id=1, source_target_pairs={{0,4},{4,8},{8,12},{12,16},{16,20},{20,24},{24,28},{28,0},{1,5},{5... | collective-permute-start | bytes 294920 | tf_op jit(solution)/shard_map/ppermute | solution.py:21
  122.1 74.9 %reduce-scatter.11.cloned.1.call-start = ((), (), s32[]{:S(2)}) async-start(), calls=%async_computation.9 | async-start | bytes 491520 | tf_op jit(solution)/shard_map/reduce_scatter | solution.py:66
  144.2 4.9 %collective-permute-start.14 = (bf16[192,256]{1,0:T(8,128)(2,1)S(1)}, bf16[192,256]{1,0:T(8,128)(2,1)S(1)}, u32[]{:S(2)}, u32[]{:S(2)}) collective-permute-start(bf16[192,256]{1,0:T(8,128)(2,1)S(1)} %get-tuple-element.332), channel_id=1, source_target_pairs={{0,4},{4,8},{8,12},{12,16},{16,20},{20,24},{24,28},{28,0},{1,5},{5... | collective-permute-start | bytes 294920 | tf_op jit(solution)/shard_map/ppermute | solution.py:21
  144.2 5.6 %collective-permute-start.15 = (bf16[192,256]{1,0:T(8,128)(2,1)S(1)}, bf16[192,256]{1,0:T(8,128)(2,1)S(1)}, u32[]{:S(2)}, u32[]{:S(2)}) collective-permute-start(bf16[192,256]{1,0:T(8,128)(2,1)S(1)} %get-tuple-element.332), channel_id=1, source_target_pairs={{0,28},{4,0},{8,4},{12,8},{16,12},{20,16},{24,20},{28,24},{1,29},{... | collective-permute-start | bytes 294920 | tf_op jit(solution)/shard_map/ppermute | solution.py:26
  149.2 4.9 %collective-permute-start.16 = (bf16[192,256]{1,0:T(8,128)(2,1)S(1)}, bf16[192,256]{1,0:T(8,128)(2,1)S(1)}, u32[]{:S(2)}, u32[]{:S(2)}) collective-permute-start(bf16[192,256]{1,0:T(8,128)(2,1)S(1)} %collective-permute-done.14), channel_id=1, source_target_pairs={{0,4},{4,8},{8,12},{12,16},{16,20},{20,24},{24,28},{28,0},{1,5},{5... | collective-permute-start | bytes 294920 | tf_op jit(solution)/shard_map/ppermute | solution.py:21
  149.8 5.1 %collective-permute-start.17 = (bf16[192,256]{1,0:T(8,128)(2,1)S(1)}, bf16[192,256]{1,0:T(8,128)(2,1)S(1)}, u32[]{:S(2)}, u32[]{:S(2)}) collective-permute-start(bf16[192,256]{1,0:T(8,128)(2,1)S(1)} %collective-permute-done.15), channel_id=1, source_target_pairs={{0,28},{4,0},{8,4},{12,8},{16,12},{20,16},{24,20},{28,24},{1,29},{... | collective-permute-start | bytes 294920 | tf_op jit(solution)/shard_map/ppermute | solution.py:26
  154.1 5.1 %collective-permute-start.18 = (bf16[192,256]{1,0:T(8,128)(2,1)S(1)}, bf16[192,256]{1,0:T(8,128)(2,1)S(1)}, u32[]{:S(2)}, u32[]{:S(2)}) collective-permute-start(bf16[192,256]{1,0:T(8,128)(2,1)S(1)} %collective-permute-done.16), channel_id=1, source_target_pairs={{0,4},{4,8},{8,12},{12,16},{16,20},{20,24},{24,28},{28,0},{1,5},{5... | collective-permute-start | bytes 294920 | tf_op jit(solution)/shard_map/ppermute | solution.py:21
  154.9 5.8 %collective-permute-start.19 = (bf16[192,256]{1,0:T(8,128)(2,1)S(1)}, bf16[192,256]{1,0:T(8,128)(2,1)S(1)}, u32[]{:S(2)}, u32[]{:S(2)}) collective-permute-start(bf16[192,256]{1,0:T(8,128)(2,1)S(1)} %collective-permute-done.17), channel_id=1, source_target_pairs={{0,28},{4,0},{8,4},{12,8},{16,12},{20,16},{24,20},{28,24},{1,29},{... | collective-permute-start | bytes 294920 | tf_op jit(solution)/shard_map/ppermute | solution.py:26
  159.2 4.9 %collective-permute-start.20 = (bf16[192,256]{1,0:T(8,128)(2,1)S(1)}, bf16[192,256]{1,0:T(8,128)(2,1)S(1)}, u32[]{:S(2)}, u32[]{:S(2)}) collective-permute-start(bf16[192,256]{1,0:T(8,128)(2,1)S(1)} %collective-permute-done.18), channel_id=1, source_target_pairs={{0,4},{4,8},{8,12},{12,16},{16,20},{20,24},{24,28},{28,0},{1,5},{5... | collective-permute-start | bytes 294920 | tf_op jit(solution)/shard_map/ppermute | solution.py:21
  177.4 75.0 %reduce-scatter.13.cloned.1.call-start = ((), (), s32[]{:S(2)}) async-start(), calls=%async_computation.10 | async-start | bytes 491520 | tf_op jit(solution)/shard_map/reduce_scatter | solution.py:66
  199.7 4.9 %collective-permute-start.21 = (bf16[192,256]{1,0:T(8,128)(2,1)S(1)}, bf16[192,256]{1,0:T(8,128)(2,1)S(1)}, u32[]{:S(2)}, u32[]{:S(2)}) collective-permute-start(bf16[192,256]{1,0:T(8,128)(2,1)S(1)} %get-tuple-element.329), channel_id=1, source_target_pairs={{0,4},{4,8},{8,12},{12,16},{16,20},{20,24},{24,28},{28,0},{1,5},{5... | collective-permute-start | bytes 294920 | tf_op jit(solution)/shard_map/ppermute | solution.py:21
  199.7 5.6 %collective-permute-start.22 = (bf16[192,256]{1,0:T(8,128)(2,1)S(1)}, bf16[192,256]{1,0:T(8,128)(2,1)S(1)}, u32[]{:S(2)}, u32[]{:S(2)}) collective-permute-start(bf16[192,256]{1,0:T(8,128)(2,1)S(1)} %get-tuple-element.329), channel_id=1, source_target_pairs={{0,28},{4,0},{8,4},{12,8},{16,12},{20,16},{24,20},{28,24},{1,29},{... | collective-permute-start | bytes 294920 | tf_op jit(solution)/shard_map/ppermute | solution.py:26
  204.6 4.9 %collective-permute-start.23 = (bf16[192,256]{1,0:T(8,128)(2,1)S(1)}, bf16[192,256]{1,0:T(8,128)(2,1)S(1)}, u32[]{:S(2)}, u32[]{:S(2)}) collective-permute-start(bf16[192,256]{1,0:T(8,128)(2,1)S(1)} %collective-permute-done.21), channel_id=1, source_target_pairs={{0,4},{4,8},{8,12},{12,16},{16,20},{20,24},{24,28},{28,0},{1,5},{5... | collective-permute-start | bytes 294920 | tf_op jit(solution)/shard_map/ppermute | solution.py:21
  205.2 5.1 %collective-permute-start.24 = (bf16[192,256]{1,0:T(8,128)(2,1)S(1)}, bf16[192,256]{1,0:T(8,128)(2,1)S(1)}, u32[]{:S(2)}, u32[]{:S(2)}) collective-permute-start(bf16[192,256]{1,0:T(8,128)(2,1)S(1)} %collective-permute-done.22), channel_id=1, source_target_pairs={{0,28},{4,0},{8,4},{12,8},{16,12},{20,16},{24,20},{28,24},{1,29},{... | collective-permute-start | bytes 294920 | tf_op jit(solution)/shard_map/ppermute | solution.py:26
  209.5 5.1 %collective-permute-start.25 = (bf16[192,256]{1,0:T(8,128)(2,1)S(1)}, bf16[192,256]{1,0:T(8,128)(2,1)S(1)}, u32[]{:S(2)}, u32[]{:S(2)}) collective-permute-start(bf16[192,256]{1,0:T(8,128)(2,1)S(1)} %collective-permute-done.23), channel_id=1, source_target_pairs={{0,4},{4,8},{8,12},{12,16},{16,20},{20,24},{24,28},{28,0},{1,5},{5... | collective-permute-start | bytes 294920 | tf_op jit(solution)/shard_map/ppermute | solution.py:21
  210.4 5.8 %collective-permute-start.26 = (bf16[192,256]{1,0:T(8,128)(2,1)S(1)}, bf16[192,256]{1,0:T(8,128)(2,1)S(1)}, u32[]{:S(2)}, u32[]{:S(2)}) collective-permute-start(bf16[192,256]{1,0:T(8,128)(2,1)S(1)} %collective-permute-done.24), channel_id=1, source_target_pairs={{0,28},{4,0},{8,4},{12,8},{16,12},{20,16},{24,20},{28,24},{1,29},{... | collective-permute-start | bytes 294920 | tf_op jit(solution)/shard_map/ppermute | solution.py:26
  214.7 4.9 %collective-permute-start.27 = (bf16[192,256]{1,0:T(8,128)(2,1)S(1)}, bf16[192,256]{1,0:T(8,128)(2,1)S(1)}, u32[]{:S(2)}, u32[]{:S(2)}) collective-permute-start(bf16[192,256]{1,0:T(8,128)(2,1)S(1)} %collective-permute-done.25), channel_id=1, source_target_pairs={{0,4},{4,8},{8,12},{12,16},{16,20},{20,24},{24,28},{28,0},{1,5},{5... | collective-permute-start | bytes 294920 | tf_op jit(solution)/shard_map/ppermute | solution.py:21
  232.8 75.0 %reduce-scatter.15.cloned.1.call-start = ((), (), s32[]{:S(2)}) async-start(), calls=%async_computation.11 | async-start | bytes 491520 | tf_op jit(solution)/shard_map/reduce_scatter | solution.py:66
  255.1 4.9 %collective-permute-start.28 = (bf16[192,256]{1,0:T(8,128)(2,1)S(1)}, bf16[192,256]{1,0:T(8,128)(2,1)S(1)}, u32[]{:S(2)}, u32[]{:S(2)}) collective-permute-start(bf16[192,256]{1,0:T(8,128)(2,1)S(1)} %get-tuple-element.326), channel_id=1, source_target_pairs={{0,4},{4,8},{8,12},{12,16},{16,20},{20,24},{24,28},{28,0},{1,5},{5... | collective-permute-start | bytes 294920 | tf_op jit(solution)/shard_map/ppermute | solution.py:21
  255.1 5.6 %collective-permute-start.29 = (bf16[192,256]{1,0:T(8,128)(2,1)S(1)}, bf16[192,256]{1,0:T(8,128)(2,1)S(1)}, u32[]{:S(2)}, u32[]{:S(2)}) collective-permute-start(bf16[192,256]{1,0:T(8,128)(2,1)S(1)} %get-tuple-element.326), channel_id=1, source_target_pairs={{0,28},{4,0},{8,4},{12,8},{16,12},{20,16},{24,20},{28,24},{1,29},{... | collective-permute-start | bytes 294920 | tf_op jit(solution)/shard_map/ppermute | solution.py:26
  260.0 4.9 %collective-permute-start.30 = (bf16[192,256]{1,0:T(8,128)(2,1)S(1)}, bf16[192,256]{1,0:T(8,128)(2,1)S(1)}, u32[]{:S(2)}, u32[]{:S(2)}) collective-permute-start(bf16[192,256]{1,0:T(8,128)(2,1)S(1)} %collective-permute-done.28), channel_id=1, source_target_pairs={{0,4},{4,8},{8,12},{12,16},{16,20},{20,24},{24,28},{28,0},{1,5},{5... | collective-permute-start | bytes 294920 | tf_op jit(solution)/shard_map/ppermute | solution.py:21
  260.7 5.1 %collective-permute-start.31 = (bf16[192,256]{1,0:T(8,128)(2,1)S(1)}, bf16[192,256]{1,0:T(8,128)(2,1)S(1)}, u32[]{:S(2)}, u32[]{:S(2)}) collective-permute-start(bf16[192,256]{1,0:T(8,128)(2,1)S(1)} %collective-permute-done.29), channel_id=1, source_target_pairs={{0,28},{4,0},{8,4},{12,8},{16,12},{20,16},{24,20},{28,24},{1,29},{... | collective-permute-start | bytes 294920 | tf_op jit(solution)/shard_map/ppermute | solution.py:26
  265.0 5.2 %collective-permute-start.32 = (bf16[192,256]{1,0:T(8,128)(2,1)S(1)}, bf16[192,256]{1,0:T(8,128)(2,1)S(1)}, u32[]{:S(2)}, u32[]{:S(2)}) collective-permute-start(bf16[192,256]{1,0:T(8,128)(2,1)S(1)} %collective-permute-done.30), channel_id=1, source_target_pairs={{0,4},{4,8},{8,12},{12,16},{16,20},{20,24},{24,28},{28,0},{1,5},{5... | collective-permute-start | bytes 294920 | tf_op jit(solution)/shard_map/ppermute | solution.py:21
  265.8 5.8 %collective-permute-start.33 = (bf16[192,256]{1,0:T(8,128)(2,1)S(1)}, bf16[192,256]{1,0:T(8,128)(2,1)S(1)}, u32[]{:S(2)}, u32[]{:S(2)}) collective-permute-start(bf16[192,256]{1,0:T(8,128)(2,1)S(1)} %collective-permute-done.31), channel_id=1, source_target_pairs={{0,28},{4,0},{8,4},{12,8},{16,12},{20,16},{24,20},{28,24},{1,29},{... | collective-permute-start | bytes 294920 | tf_op jit(solution)/shard_map/ppermute | solution.py:26
  270.1 4.9 %collective-permute-start.34 = (bf16[192,256]{1,0:T(8,128)(2,1)S(1)}, bf16[192,256]{1,0:T(8,128)(2,1)S(1)}, u32[]{:S(2)}, u32[]{:S(2)}) collective-permute-start(bf16[192,256]{1,0:T(8,128)(2,1)S(1)} %collective-permute-done.32), channel_id=1, source_target_pairs={{0,4},{4,8},{8,12},{12,16},{16,20},{20,24},{24,28},{28,0},{1,5},{5... | collective-permute-start | bytes 294920 | tf_op jit(solution)/shard_map/ppermute | solution.py:21
  288.3 72.7 %reduce-scatter.17.cloned.1.call-start = ((), (), s32[]{:S(2)}) async-start(), calls=%async_computation.12 | async-start | bytes 491520 | tf_op jit(solution)/shard_map/reduce_scatter | solution.py:66
  308.9 5.0 %collective-permute-start.35 = (bf16[192,256]{1,0:T(8,128)(2,1)S(1)}, bf16[192,256]{1,0:T(8,128)(2,1)S(1)}, u32[]{:S(2)}, u32[]{:S(2)}) collective-permute-start(bf16[192,256]{1,0:T(8,128)(2,1)S(1)} %get-tuple-element.324), channel_id=1, source_target_pairs={{0,4},{4,8},{8,12},{12,16},{16,20},{20,24},{24,28},{28,0},{1,5},{5... | collective-permute-start | bytes 294920 | tf_op jit(solution)/shard_map/ppermute | solution.py:21
  309.0 4.9 %collective-permute-start.36 = (bf16[192,256]{1,0:T(8,128)(2,1)S(1)}, bf16[192,256]{1,0:T(8,128)(2,1)S(1)}, u32[]{:S(2)}, u32[]{:S(2)}) collective-permute-start(bf16[192,256]{1,0:T(8,128)(2,1)S(1)} %get-tuple-element.324), channel_id=1, source_target_pairs={{0,28},{4,0},{8,4},{12,8},{16,12},{20,16},{24,20},{28,24},{1,29},{... | collective-permute-start | bytes 294920 | tf_op jit(solution)/shard_map/ppermute | solution.py:26
  313.9 5.2 %collective-permute-start.37 = (bf16[192,256]{1,0:T(8,128)(2,1)S(1)}, bf16[192,256]{1,0:T(8,128)(2,1)S(1)}, u32[]{:S(2)}, u32[]{:S(2)}) collective-permute-start(bf16[192,256]{1,0:T(8,128)(2,1)S(1)} %collective-permute-done.35), channel_id=1, source_target_pairs={{0,4},{4,8},{8,12},{12,16},{16,20},{20,24},{24,28},{28,0},{1,5},{5... | collective-permute-start | bytes 294920 | tf_op jit(solution)/shard_map/ppermute | solution.py:21
  313.9 5.2 %collective-permute-start.38 = (bf16[192,256]{1,0:T(8,128)(2,1)S(1)}, bf16[192,256]{1,0:T(8,128)(2,1)S(1)}, u32[]{:S(2)}, u32[]{:S(2)}) collective-permute-start(bf16[192,256]{1,0:T(8,128)(2,1)S(1)} %collective-permute-done.36), channel_id=1, source_target_pairs={{0,28},{4,0},{8,4},{12,8},{16,12},{20,16},{24,20},{28,24},{1,29},{... | collective-permute-start | bytes 294920 | tf_op jit(solution)/shard_map/ppermute | solution.py:26
  319.1 5.8 %collective-permute-start.39 = (bf16[192,256]{1,0:T(8,128)(2,1)S(1)}, bf16[192,256]{1,0:T(8,128)(2,1)S(1)}, u32[]{:S(2)}, u32[]{:S(2)}) collective-permute-start(bf16[192,256]{1,0:T(8,128)(2,1)S(1)} %collective-permute-done.37), channel_id=1, source_target_pairs={{0,4},{4,8},{8,12},{12,16},{16,20},{20,24},{24,28},{28,0},{1,5},{5... | collective-permute-start | bytes 294920 | tf_op jit(solution)/shard_map/ppermute | solution.py:21
  319.1 5.9 %collective-permute-start.40 = (bf16[192,256]{1,0:T(8,128)(2,1)S(1)}, bf16[192,256]{1,0:T(8,128)(2,1)S(1)}, u32[]{:S(2)}, u32[]{:S(2)}) collective-permute-start(bf16[192,256]{1,0:T(8,128)(2,1)S(1)} %collective-permute-done.38), channel_id=1, source_target_pairs={{0,28},{4,0},{8,4},{12,8},{16,12},{20,16},{24,20},{28,24},{1,29},{... | collective-permute-start | bytes 294920 | tf_op jit(solution)/shard_map/ppermute | solution.py:26
  (7 other events, 83.8 us)
Sparse Core Ops, SparseCore 0:
  65.4 21.0 reduce-scatter.6
  122.2 19.4 reduce-scatter.8
  177.5 19.4 reduce-scatter.10
  233.0 19.3 reduce-scatter.12
  288.4 19.4 reduce-scatter.14
  342.8 18.0 reduce-scatter.16
